TPU v7x, 512 devices: a whole 4x8x8 slice. The times are simulated.
512 devices in a mesh: dp: 64 (over y, z), fsdp: 8 (over x, core).
Axes of the slice: x: 4, y: 8, z: 8, core: 2. Of those that a mesh axis runs over, the one named last changes fastest.
Arguments:
- frames: bfloat16 [524288, 512], P(('dp', 'fsdp')), may hold values from -6 to 6
- utt_pairs: int32 [8, 64, 4], P('fsdp'), may hold values from 32 to 256, as said below
- utt_dest: int32 [8, 64, 4], P('fsdp'), may hold values from 0 to 63, as said below
- conv_weight: bfloat16 [1536, 512], P('dp'), may hold values from -0.15625 to 0.15625
- proj_weight: bfloat16 [512, 1536], P('dp'), may hold values from -0.25 to 0.25
- point_weight: bfloat16 [2, 1536, 1536], P(None, None, 'fsdp'), may hold values from -0.15625 to 0.15625
- depth_weight: float32 [31, 1536], replicated, may hold values from -1 to 1
- gain_first: float32 [1536], replicated, may hold values from 0.5 to 1.5
- gain_second: float32 [1536], replicated, may hold values from 0.5 to 1.5
Outputs:
- encoded: bfloat16 [262144, 1536], P(('dp', 'fsdp'))
Inputs may be any that keep to these rules, and one draw needn't show every extreme that they name: `utt_pairs`: every loader holds exactly 512 pairs and every sequence device receives exactly 512 pairs, from 4 different loaders. Each loader holds one utterance of exactly 256 pairs and one of exactly 32 pairs. `utt_dest`: the 4 utterances of loader i go to the 4 different sequence devices (i + k * 64 / 4) mod 64, k = 0 .. 3, in some order.
All inputs are finite; a program needn't handle non-finite values.
Results may differ from a plain program's by a relative error of at most 0.012.
Values may be sent and summed in bfloat16 or wider, within the bound.
No kernel may reach another device: no remote copies, remote signals or barrier semaphores. Data moves between devices by JAX's collectives and lax.ppermute only.
A program may use at most 64 MiB of HBM per device.

v0:
```python
import jax
import jax.numpy as jnp
from jax import lax
from jax.sharding import PartitionSpec as P


def passed_along(value, axis, steps):
    count = lax.axis_size(axis)
    pairs = [(source, (source + steps) % count) for source in range(count)]
    return lax.ppermute(value, axis, pairs)


def frontend(pair_rows, first_rows, conv_full):
    channels = pair_rows.shape[1] // 2
    even_frames = pair_rows[:, :channels]
    odd_frames = pair_rows[:, channels:]
    earlier = jnp.pad(odd_frames[:-1], ((1, 0), (0, 0)))
    earlier = jnp.where(first_rows[:, None], jnp.zeros_like(earlier), earlier)
    summed = jnp.dot(earlier, conv_full[:channels], preferred_element_type=jnp.float32)
    summed = summed + jnp.dot(
        even_frames, conv_full[channels : 2 * channels], preferred_element_type=jnp.float32
    )
    summed = summed + jnp.dot(
        odd_frames, conv_full[2 * channels :], preferred_element_type=jnp.float32
    )
    return jax.nn.relu(summed).astype(jnp.bfloat16)


def layer_norm(values, scales):
    centered = values - jnp.mean(values, axis=-1, keepdims=True)
    variance = jnp.mean(centered * centered, axis=-1, keepdims=True)
    return centered * lax.rsqrt(variance + 1e-05) * scales


def depthwise(gated, depth_weight, positions, lengths):
    row_count = gated.shape[0]
    kernel_size = depth_weight.shape[0]
    half_width = kernel_size // 2
    padded = jnp.pad(gated.astype(jnp.float32), ((half_width, half_width), (0, 0)))
    mixed = jnp.zeros(gated.shape, jnp.float32)
    for tap_index in range(kernel_size):
        offset = tap_index - half_width
        inside = (positions + offset >= 0) & (positions + offset < lengths)
        term = padded[tap_index : tap_index + row_count] * depth_weight[tap_index][None, :]
        mixed = mixed + jnp.where(inside[:, None], term, jnp.zeros_like(term))
    return mixed


def gate_product(normed, value_weight, gate_weight):
    value_part = jnp.dot(normed, value_weight, preferred_element_type=jnp.float32)
    gate_part = jnp.dot(normed, gate_weight, preferred_element_type=jnp.float32)
    return (value_part * jax.nn.sigmoid(gate_part)).astype(jnp.bfloat16)


def cut_pieces(source_rows, own_starts, slot_size, utt_count):
    padded = jnp.pad(source_rows, ((0, slot_size), (0, 0)))
    pieces = []
    for slot_index in range(utt_count):
        pieces.append(lax.dynamic_slice_in_dim(padded, own_starts[slot_index], slot_size, 0))
    return pieces


def body(
    frames,
    utt_pairs,
    utt_dest,
    conv_weight,
    proj_weight,
    point_weight,
    depth_weight,
    gain_first,
    gain_second,
):
    node_count = lax.axis_size("dp")
    own_index = lax.axis_index("dp")
    pair_count = frames.shape[0] // 2
    channels = frames.shape[1]
    utt_count = utt_pairs.shape[2]
    spacing = node_count // utt_count
    slot_size = pair_count // 2
    pair_table = utt_pairs[0]
    dest_table = utt_dest[0]
    loader_ids = jnp.arange(node_count, dtype=jnp.int32)
    slot_ids = jnp.arange(utt_count, dtype=jnp.int32)
    slot_table = (dest_table - loader_ids[:, None]) % node_count // spacing
    matches = (slot_table[:, :, None] == slot_ids[None, None, :]).astype(jnp.int32)
    loader_offsets = jnp.cumsum(pair_table, axis=1) - pair_table
    slot_counts = jnp.sum(matches * pair_table[:, :, None], axis=1)
    slot_starts = jnp.sum(matches * loader_offsets[:, :, None], axis=1)
    conv_full, proj_full = (
        lax.all_gather(conv_weight, "dp", axis=0, tiled=True),
        lax.all_gather(proj_weight, "dp", axis=0, tiled=True),
    )
    own_starts = slot_starts[own_index]
    sources = (own_index - slot_ids * spacing) % node_count
    piece_lengths = slot_counts[sources, slot_ids]
    earlier_pieces = (sources[None, :] < sources[:, None]).astype(jnp.int32)
    piece_offsets = jnp.sum(earlier_pieces * piece_lengths[None, :], axis=1)
    pair_rows = jnp.arange(pair_count, dtype=jnp.int32)
    inside = (
        (pair_rows[:, None] >= piece_offsets[None, :])
        & (pair_rows[:, None] < piece_offsets[None, :] + piece_lengths[None, :])
    ).astype(jnp.int32)
    piece_index = jnp.sum(inside * slot_ids[None, :], axis=1)
    positions = pair_rows - jnp.sum(inside * piece_offsets[None, :], axis=1)
    lengths = jnp.sum(inside * piece_lengths[None, :], axis=1)
    flat_slot = piece_index * slot_size + positions
    frame_pairs = frames.reshape(pair_count, 2 * channels)
    pieces = cut_pieces(frame_pairs, own_starts, slot_size, utt_count)
    arrived = [pieces[0]]
    for slot_index in range(1, utt_count):
        arrived.append(passed_along(pieces[slot_index], "dp", slot_index * spacing))
    stacked = jnp.concatenate(arrived, axis=0)
    packed = jnp.take(stacked, flat_slot, axis=0)
    front = frontend(packed, positions == 0, conv_full)
    projected = jnp.dot(front, proj_full, preferred_element_type=jnp.float32).astype(jnp.bfloat16)
    normed = layer_norm(projected.astype(jnp.float32), gain_first).astype(jnp.bfloat16)
    weight_part = lax.all_gather(point_weight, "fsdp", axis=2, tiled=True)
    gated = gate_product(normed, weight_part[0], weight_part[1])
    mixed = depthwise(gated, depth_weight, positions, lengths)
    scaled = layer_norm(mixed, gain_second)
    return (scaled * jax.nn.sigmoid(scaled)).astype(jnp.bfloat16)


def solution(mesh):
    in_specs = (
        P(("dp", "fsdp"), None),
        P("fsdp", None, None),
        P("fsdp", None, None),
        P("dp", None),
        P("dp", None),
        P(None, None, "fsdp"),
        P(),
        P(),
        P(),
    )
    out_specs = P(("dp", "fsdp"), None)
    return jax.shard_map(body, mesh=mesh, in_specs=in_specs, out_specs=out_specs, check_vma=False)
```

profile of v0, /device:TPU:1, one launch (start us, length us, event | category | flops | bytes accessed | tf_op | source)
XLA Modules:
  0.0 303.4 jit_solution(6321874885541037050)
XLA Ops:
  6.5 0.7 all-gather.4.cloned.1.call-update
  8.8 0.8 reduce_window_sum.11
  9.5 0.7 add_select_fusion
  16.7 1.4 reshape.518
  20.7 1.6 pad_dynamic-slice_fusion.3
  22.2 5.1 %collective-permute-start = (bf16[256,1024]{1,0:T(8,128)(2,1)S(1)}, bf16[256,1024]{1,0:T(8,128)(2,1)S(1)}, u32[]{:S(2)}, u32[]{:S(2)}) collective-permute-start(bf16[256,1024]{1,0:T(8,128)(2,1)S(1)} %get-tuple-element.44), channel_id=1, source_target_pairs={{0,128},{8,136},{16,144},{24,152},{32,160},{40,168},{48,176},{56,1... | collective-permute-start | bytes 1572872 | tf_op jit(solution)/shard_map/ppermute | solution.py:10
  27.3 5.7 %collective-permute-start.1 = (bf16[256,1024]{1,0:T(8,128)(2,1)S(1)}, bf16[256,1024]{1,0:T(8,128)(2,1)}, u32[]{:S(2)}, u32[]{:S(2)}) collective-permute-start(bf16[256,1024]{1,0:T(8,128)(2,1)S(1)} %get-tuple-element.45), channel_id=1, source_target_pairs={{0,256},{8,264},{16,272},{24,280},{32,288},{40,296},{48,304},{56,3... | collective-permute-start | bytes 1572872 | tf_op jit(solution)/shard_map/ppermute | solution.py:10
  33.0 5.0 %collective-permute-start.2 = (bf16[256,1024]{1,0:T(8,128)(2,1)S(1)}, bf16[256,1024]{1,0:T(8,128)(2,1)}, u32[]{:S(2)}, u32[]{:S(2)}) collective-permute-start(bf16[256,1024]{1,0:T(8,128)(2,1)S(1)} %get-tuple-element.46), channel_id=1, source_target_pairs={{0,384},{8,392},{16,400},{24,408},{32,416},{40,424},{48,432},{56,4... | collective-permute-start | bytes 1572872 | tf_op jit(solution)/shard_map/ppermute | solution.py:10
  39.0 0.8 slice_reduce_fusion.29
  40.2 1.1 collective-permute-done
  41.2 27.6 %collective-permute-done.1 = bf16[256,1024]{1,0:T(8,128)(2,1)} collective-permute-done((bf16[256,1024]{1,0:T(8,128)(2,1)S(1)}, bf16[256,1024]{1,0:T(8,128)(2,1)}, u32[]{:S(2)}, u32[]{:S(2)}) %collective-permute-start.1) | collective-permute-done | bytes 524320 | tf_op jit(solution)/shard_map/ppermute | solution.py:10
  68.8 11.9 %collective-permute-done.2 = bf16[256,1024]{1,0:T(8,128)(2,1)} collective-permute-done((bf16[256,1024]{1,0:T(8,128)(2,1)S(1)}, bf16[256,1024]{1,0:T(8,128)(2,1)}, u32[]{:S(2)}, u32[]{:S(2)}) %collective-permute-start.2) | collective-permute-done | bytes 524320 | tf_op jit(solution)/shard_map/ppermute | solution.py:10
  80.7 1.5 pad_maximum_fusion
  82.3 2.2 gather_fusion.1
  84.7 31.2 %all-gather.4.cloned.1.call-done = bf16[1536,512]{1,0:T(8,128)(2,1)} async-done(((bf16[24,512]{1,0:T(8,128)(2,1)}), bf16[1536,512]{1,0:T(8,128)(2,1)}) %all-gather.4.cloned.1.call-update) | async-done | bytes 1572880 | tf_op jit(solution)/shard_map/all_gather | solution.py:91
  116.0 1.5 fusion.62
  117.5 2.5 convolution_add_fusion.1
  120.0 78.9 %all-gather.6.cloned.1.call-done = bf16[512,1536]{1,0:T(8,128)(2,1)} async-done(((bf16[8,1536]{1,0:T(8,128)(2,1)}), bf16[512,1536]{1,0:T(8,128)(2,1)}) %all-gather.6.cloned.1.call-update) | async-done | bytes 1572880 | tf_op jit(solution)/shard_map/all_gather | solution.py:92
  198.9 3.2 %convert_reduce_fusion = (f32[512]{0:T(512)S(1)}, bf16[512,1536]{1,0:T(8,128)(2,1)S(1)}) fusion(bf16[512,1536]{1,0:T(8,128)(2,1)} %all-gather.6.cloned.1.call-done, f32[512,512]{1,0:T(8,128)} %convolution_add_fusion.1, bf16[1536,512]{1,0:T(8,128)(2,1)} %all-gather.4.cloned.1.call-done, bf16[512,1024]{1,0:T(8,128)(2,1)S(1)} %broadcast_select_fusion), kind=kOutput, calls=%fused_computation.7 | convolution fusion | flops 1076887040 | bytes 5244928 | tf_op jit(solution)/shard_map/dot_general | solution.py:116
  202.7 59.3 %all-gather.8.cloned.1.call-done = bf16[2,1536,1536]{1,2,0:T(8,128)(2,1)} async-done(((bf16[2,1536,192]{1,2,0:T(8,128)(2,1)}), bf16[2,1536,1536]{1,2,0:T(8,128)(2,1)}) %all-gather.8.cloned.1.call-update) | async-done | bytes 9437200 | tf_op jit(solution)/shard_map/all_gather | solution.py:118
  261.9 5.2 %fusion.7 = f32[512,1536]{1,0:T(8,128)S(1)} fusion(bf16[2,1536,1536]{1,2,0:T(8,128)(2,1)} %all-gather.8.cloned.1.call-done, bf16[512,1536]{1,0:T(8,128)(2,1)S(1)} %get-tuple-element.85, f32[1536]{0:T(1024)S(1)} %copy-done.10, f32[512]{0:T(512)S(1)} %add_rsqrt_fusion.1, f32[512]{0:T(512)S(1)} %broadcast_multiply_fusion.1), kind=kOutput, calls=%fused_computation.13 | convolution fusion | flops 2421424128 | bytes 9447424 | tf_op jit(solution)/shard_map/dot_general | solution.py:51
  267.2 2.7 fusion.53
  269.9 24.0 %fusion.83 = (f32[512]{0:T(512)S(1)}, f32[512,1536]{1,0:T(8,128)S(1)}) fusion(f32[1536]{0:T(1024)S(1)} %copy-done.6, pred[512]{0:T(512)(128)(4,1)S(1)} %get-tuple-element.48, f32[1536]{0:T(1024)S(1)} %copy-done.7, pred[512]{0:T(512)(128)(4,1)S(1)} %get-tuple-element.49, f32[1536]{0:T(1024)S(1)} %get-tuple-element.6, ...), kind=kLoop, calls=%fused_computation.211 | loop fusion | flops 73137664 | bytes 6499840 | tf_op jit(solution)/shard_map/reduce_sum | solution.py:30
  294.6 2.2 multiply_convert_fusion
  (49 shorter events, 5.7 us)
Async XLA Ops:
  6.5 109.4 %all-gather.4.cloned.1.call-start = ((), (), s32[]{:S(2)}) async-start(), calls=%async_computation | async-start | bytes 1597440 | tf_op jit(solution)/shard_map/all_gather | solution.py:91
  7.3 191.6 %all-gather.6.cloned.1.call-start = ((), (), s32[]{:S(2)}) async-start(), calls=%async_computation.1 | async-start | bytes 1597440 | tf_op jit(solution)/shard_map/all_gather | solution.py:92
  8.0 253.9 %all-gather.8.cloned.1.call-start = ((), (), s32[]{:S(2)}) async-start(), calls=%async_computation.2 | async-start | bytes 10616832 | tf_op jit(solution)/shard_map/all_gather | solution.py:118
  8.7 30.2 %copy-start.1 = (f32[31,1536]{1,0:T(8,128)S(1)}, f32[31,1536]{1,0:T(8,128)}, u32[]{:S(2)}) copy-start(f32[31,1536]{1,0:T(8,128)} %param.15) | copy-start | bytes 571396
  22.2 19.0 %collective-permute-start = (bf16[256,1024]{1,0:T(8,128)(2,1)S(1)}, bf16[256,1024]{1,0:T(8,128)(2,1)S(1)}, u32[]{:S(2)}, u32[]{:S(2)}) collective-permute-start(bf16[256,1024]{1,0:T(8,128)(2,1)S(1)} %get-tuple-element.44), channel_id=1, source_target_pairs={{0,128},{8,136},{16,144},{24,152},{32,160},{40,168},{48,176},{56,1... | collective-permute-start | bytes 1572872 | tf_op jit(solution)/shard_map/ppermute | solution.py:10
  27.3 41.5 %collective-permute-start.1 = (bf16[256,1024]{1,0:T(8,128)(2,1)S(1)}, bf16[256,1024]{1,0:T(8,128)(2,1)}, u32[]{:S(2)}, u32[]{:S(2)}) collective-permute-start(bf16[256,1024]{1,0:T(8,128)(2,1)S(1)} %get-tuple-element.45), channel_id=1, source_target_pairs={{0,256},{8,264},{16,272},{24,280},{32,288},{40,296},{48,304},{56,3... | collective-permute-start | bytes 1572872 | tf_op jit(solution)/shard_map/ppermute | solution.py:10
  33.0 47.8 %collective-permute-start.2 = (bf16[256,1024]{1,0:T(8,128)(2,1)S(1)}, bf16[256,1024]{1,0:T(8,128)(2,1)}, u32[]{:S(2)}, u32[]{:S(2)}) collective-permute-start(bf16[256,1024]{1,0:T(8,128)(2,1)S(1)} %get-tuple-element.46), channel_id=1, source_target_pairs={{0,384},{8,392},{16,400},{24,408},{32,416},{40,424},{48,432},{56,4... | collective-permute-start | bytes 1572872 | tf_op jit(solution)/shard_map/ppermute | solution.py:10
  41.2 39.5 %copy-start = (bf16[256,1024]{1,0:T(8,128)(2,1)}, bf16[256,1024]{1,0:T(8,128)(2,1)S(1)}, u32[]{:S(2)}) copy-start(bf16[256,1024]{1,0:T(8,128)(2,1)S(1)} %collective-permute-done) | copy-start | bytes 1572868
  120.0 142.0 %copy-start.10 = (f32[1536]{0:T(1024)S(1)}, f32[1536]{0:T(1024)}, u32[]{:S(2)}) copy-start(f32[1536]{0:T(1024)} %param.16) | copy-start | bytes 18436
  261.9 5.2 %copy-start.9 = (bf16[2,1536,1536]{1,2,0:T(8,128)(2,1)S(1)}, bf16[2,1536,1536]{1,2,0:T(8,128)(2,1)}, u32[]{:S(2)}) copy-start(bf16[2,1536,1536]{1,2,0:T(8,128)(2,1)} %all-gather.8.cloned.1.call-done) | copy-start | bytes 28311556
  267.1 2.8 copy-start.2
  267.1 2.8 copy-start.3
  267.1 2.8 copy-start.4
  267.2 2.8 copy-start.5
  267.2 2.8 copy-start.6
  267.2 2.8 copy-start.7
  293.9 0.7 copy-start.8
Sparse Core Ops, SparseCore 0:
  10.4 105.5 all-gather.3
  119.0 79.7 all-gather.5
  201.0 60.9 all-gather.7
where the time goes:
time: 304 us; the launch traced here: 303 us
  waiting for transfers between devices  212 us (70%)
  other arithmetic  31.5 us (10%)
  between operations  21 us (7%)
  starting transfers between devices  15.8 us (5%)
  matrix products  15 us (5%)
  local copies, waits for them, and re-layouts  7.95 us (3%)
    all_gather x1, waiting for transfers between devices, body(): lax.all_gather(proj_weight, 'dp', axis=0, tiled=True)  78.9 us
    all_gather x1, waiting for transfers between devices, body(): weight_part = lax.all_gather(point_weight, 'fsdp', axis=2, tiled=True)  59.3 us
    ppermute x3, waiting for transfers between devices, passed_along(): return lax.ppermute(value, axis, pairs)  40.6 us
    all_gather x1, waiting for transfers between devices, body(): lax.all_gather(conv_weight, 'dp', axis=0, tiled=True)  31.2 us
    reduce_sum x1, other arithmetic, layer_norm(): centered = values - jnp.mean(values, axis=-1, keepdims=True)  24 us
    ppermute x3, starting transfers between devices, passed_along(): return lax.ppermute(value, axis, pairs)  15.7 us
  transfers between devices with their start and end apart: 6, of which 6 were waited for; matrix products, arithmetic and copies ran while one was open for 7% of the time, Pallas kernels for 0%

commit v1 on v0

--- a/solution.py
+++ b/solution.py
@@ -115,7 +115,11 @@
     front = frontend(packed, positions == 0, conv_full)
     projected = jnp.dot(front, proj_full, preferred_element_type=jnp.float32).astype(jnp.bfloat16)
     normed = layer_norm(projected.astype(jnp.float32), gain_first).astype(jnp.bfloat16)
-    weight_part = lax.all_gather(point_weight, "fsdp", axis=2, tiled=True)
+    peers = lax.axis_size("fsdp")
+    repeats = [peers if d == 2 else 1 for d in range(point_weight.ndim)]
+    weight_part = lax.all_to_all(
+        jnp.tile(point_weight, repeats), "fsdp", split_axis=2, concat_axis=2, tiled=True
+    )
     gated = gate_product(normed, weight_part[0], weight_part[1])
     mixed = depthwise(gated, depth_weight, positions, lengths)
     scaled = layer_norm(mixed, gain_second)

time: 304 us -> 377 us (1.24); the launches traced: 303 us -> 372 us
  local copies, waits for them, and re-layouts: 7.95 us -> 126 us
  waiting for transfers between devices: 212 us -> 159 us
  starting transfers between devices: 15.8 us -> 20.4 us
    all_gather x1 -> x0, waiting for transfers between devices: 59.3 us -> none  [body(): weight_part = lax.all_gather(point_weight, 'fsdp', axis=2, tiled=True)]
    another operation x0 -> x2, local copies, waits for them, and re-layouts: none -> 54.3 us  [body(): jnp.tile(point_weight, repeats)]
    unnamed x22 -> x32, local copies, waits for them, and re-layouts: 0.26 us -> 45.1 us
    slice x0 -> x1, local copies, waits for them, and re-layouts: none -> 19.6 us  [body(): gated = gate_product(normed, weight_part[0], weight_part[1])]
    all_gather x1, waiting for transfers between devices: 31.2 us -> 45 us  [body(): lax.all_gather(conv_weight, 'dp', axis=0, tiled=True)]
    all_to_all x0 -> x1, starting transfers between devices: none -> 11.9 us  [body(): lax.all_to_all(jnp.tile(point_weight, repeats), 'fsdp', split_axis=2, con...]
    ppermute x3, starting transfers between devices: 15.7 us -> 8.43 us  [passed_along(): return lax.ppermute(value, axis, pairs)]
    ppermute x3, waiting for transfers between devices: 40.6 us -> 34.7 us  [passed_along(): return lax.ppermute(value, axis, pairs)]
  transfers between devices with their start and end apart: 6 -> 6, of which waited for: 6 -> 4; matrix products, arithmetic and copies ran while one was open for 7% -> 5% of each run, Pallas kernels for 0% -> 0%
where the time goes in v1:
time: 377 us; the launch traced here: 372 us
  waiting for transfers between devices  159 us (42%)
  local copies, waits for them, and re-layouts  126 us (33%)
  other arithmetic  30 us (8%)
  between operations  21.1 us (6%)
  starting transfers between devices  20.4 us (5%)
  matrix products  15 us (4%)
    all_gather x1, waiting for transfers between devices, body(): lax.all_gather(proj_weight, 'dp', axis=0, tiled=True)  78.4 us
    another operation x2, local copies, waits for them, and re-layouts, body(): jnp.tile(point_weight, repeats)  54.3 us
    unnamed x32, local copies, waits for them, and re-layouts  45.1 us
    all_gather x1, waiting for transfers between devices, body(): lax.all_gather(conv_weight, 'dp', axis=0, tiled=True)  45 us
    ppermute x3, waiting for transfers between devices, passed_along(): return lax.ppermute(value, axis, pairs)  34.7 us
    reduce_sum x1, other arithmetic, layer_norm(): centered = values - jnp.mean(values, axis=-1, keepdims=True)  23.9 us
    slice x1, local copies, waits for them, and re-layouts, body(): gated = gate_product(normed, weight_part[0], weight_part[1])  19.6 us
    all_to_all x1, starting transfers between devices, body(): lax.all_to_all(jnp.tile(point_weight, repeats), 'fsdp', split_axis=2, con...  11.9 us
  transfers between devices with their start and end apart: 6, of which 4 were waited for; matrix products, arithmetic and copies ran while one was open for 5% of the time, Pallas kernels for 0%

profile of v1, /device:TPU:1, one launch (start us, length us, event | category | flops | bytes accessed | tf_op | source)
XLA Modules:
  0.0 372.2 jit_solution(3981288067965822712)
XLA Ops:
  6.5 2.2 tile.4
  8.7 52.2 %copy.31 = bf16[2,1536,1536]{1,0,2:T(2,128)(2,1)} copy(bf16[2,1536,1536]{1,2,0:T(8,128)(2,1)S(1)} %bitcast.41) | data formatting | bytes 18874368 | tf_op jit(solution)/shard_map/tile | solution.py:121
  60.9 11.9 %all-to-all-start = ((bf16[2,1536,1536]{1,0,2:T(2,128)(2,1)}), bf16[2,1536,1536]{1,0,2:T(2,128)(2,1)}, u32[]{:S(2)}, u32[]{:S(2)}) async-start(bf16[2,1536,1536]{1,0,2:T(2,128)(2,1)} %copy.31), calls=%async_computation | async-start | bytes 18874368 | tf_op jit(solution)/shard_map/all_to_all | solution.py:120
  82.9 2.4 pad_dynamic-slice_fusion.3
  85.3 1.9 collective-permute-start.2
  87.2 2.1 collective-permute-start.1
  89.3 4.4 %collective-permute-start = (bf16[256,1024]{1,0:T(8,128)(2,1)S(1)}, bf16[256,1024]{1,0:T(8,128)(2,1)}, u32[]{:S(2)}, u32[]{:S(2)}) collective-permute-start(bf16[256,1024]{1,0:T(8,128)(2,1)S(1)} %get-tuple-element.46), channel_id=1, source_target_pairs={{0,128},{8,136},{16,144},{24,152},{32,160},{40,168},{48,176},{56,1... | collective-permute-start | bytes 1572872 | tf_op jit(solution)/shard_map/ppermute | solution.py:10
  95.3 0.8 slice_reduce_fusion.29
  96.5 31.2 %collective-permute-done.2 = bf16[256,1024]{1,0:T(8,128)(2,1)S(1)} collective-permute-done((bf16[256,1024]{1,0:T(8,128)(2,1)}, bf16[256,1024]{1,0:T(8,128)(2,1)S(1)}, u32[]{:S(2)}, u32[]{:S(2)}) %collective-permute-start.2) | collective-permute-done | bytes 524320 | tf_op jit(solution)/shard_map/ppermute | solution.py:10
  127.7 3.5 collective-permute-done
  131.2 1.5 pad_maximum_fusion
  132.8 2.1 gather_fusion.1
  135.0 45.0 %all-gather.3.cloned.1.call-done = bf16[1536,512]{1,0:T(8,128)(2,1)} async-done(((bf16[24,512]{1,0:T(8,128)(2,1)}), bf16[1536,512]{1,0:T(8,128)(2,1)}) %all-gather.3.cloned.1.call-update) | async-done | bytes 1572880 | tf_op jit(solution)/shard_map/all_gather | solution.py:91
  180.0 1.5 fusion.79
  181.5 2.5 convolution_add_fusion.1
  184.0 78.4 %all-gather.5.cloned.1.call-done = bf16[512,1536]{1,0:T(8,128)(2,1)} async-done(((bf16[8,1536]{1,0:T(8,128)(2,1)}), bf16[512,1536]{1,0:T(8,128)(2,1)}) %all-gather.5.cloned.1.call-update) | async-done | bytes 1572880 | tf_op jit(solution)/shard_map/all_gather | solution.py:92
  262.4 3.2 convert_reduce_fusion
  266.2 19.6 %fusion.101 = (bf16[1,1536,1536]{1,0,2:T(2,128)(2,1)}, bf16[1,1536,1536]{1,0,2:T(2,128)(2,1)}) fusion(bf16[2,1536,1536]{1,0,2:T(2,128)(2,1)} %all-to-all-done), kind=kLoop, calls=%fused_computation.213 | loop fusion | bytes 18874368 | tf_op jit(solution)/shard_map/slice | solution.py:123
  285.7 22.4 %copy.35 = bf16[1,1536,1536]{2,1,0:T(8,128)(2,1)} copy(bf16[1,1536,1536]{1,0,2:T(2,128)(2,1)} %get-tuple-element.44) | data formatting | bytes 9437184
  308.1 22.4 %copy.34 = bf16[1,1536,1536]{2,1,0:T(8,128)(2,1)} copy(bf16[1,1536,1536]{1,0,2:T(2,128)(2,1)} %get-tuple-element.43) | data formatting | bytes 9437184
  330.6 5.1 %fusion.18 = f32[512,1536]{1,0:T(8,128)S(1)} fusion(bf16[1,1536,1536]{2,1,0:T(8,128)(2,1)} %copy.35, bf16[512,1536]{1,0:T(8,128)(2,1)S(1)} %get-tuple-element.87, f32[1536]{0:T(1024)S(1)} %copy-done.14, f32[512]{0:T(512)S(1)} %add_rsqrt_fusion.1, f32[512]{0:T(512)S(1)} %broadcast_multiply_fusion.1), kind=kOutput, calls=%fused_computation.14 | convolution fusion | flops 2422210560 | bytes 9447424 | tf_op jit(solution)/shard_map/dot_general | solution.py:51
  335.8 2.7 fusion.68
  338.5 23.9 %fusion.100 = (f32[512]{0:T(512)S(1)}, f32[512,1536]{1,0:T(8,128)S(1)}) fusion(f32[1536]{0:T(1024)S(1)} %copy-done.8, pred[512]{0:T(512)(128)(4,1)S(1)} %get-tuple-element.50, f32[1536]{0:T(1024)S(1)} %copy-done.9, pred[512]{0:T(512)(128)(4,1)S(1)} %get-tuple-element.51, f32[1536]{0:T(1024)S(1)} %get-tuple-element.6, ...), kind=kLoop, calls=%fused_computation.212 | loop fusion | flops 73137664 | bytes 6499840 | tf_op jit(solution)/shard_map/reduce_sum | solution.py:30
  363.1 2.2 multiply_convert_fusion
  (61 shorter events, 6.0 us)
Async XLA Ops:
  60.9 13.4 %copy-start.10 = (s32[1,64,4]{1,2,0:T(4,128)S(1)}, s32[1,64,4]{1,2,0:T(4,128)}, u32[]{:S(2)}) copy-start(s32[1,64,4]{1,2,0:T(4,128)} %param.10) | copy-start | bytes 3076
  60.9 13.5 %copy-start.13 = (s32[1,64,4]{1,2,0:T(4,128)S(1)}, s32[1,64,4]{1,2,0:T(4,128)}, u32[]{:S(2)}) copy-start(s32[1,64,4]{1,2,0:T(4,128)} %param.11) | copy-start | bytes 3076
  60.9 19.1 %copy-start.1 = (bf16[1024,512]{1,0:T(8,128)(2,1)S(1)}, bf16[1024,512]{1,0:T(8,128)(2,1)}, u32[]{:S(2)}) copy-start(bf16[1024,512]{1,0:T(8,128)(2,1)} %param.9) | copy-start | bytes 3145732
  60.9 205.3 %all-to-all-start = ((bf16[2,1536,1536]{1,0,2:T(2,128)(2,1)}), bf16[2,1536,1536]{1,0,2:T(2,128)(2,1)}, u32[]{:S(2)}, u32[]{:S(2)}) async-start(bf16[2,1536,1536]{1,0,2:T(2,128)(2,1)} %copy.31), calls=%async_computation | async-start | bytes 18874368 | tf_op jit(solution)/shard_map/all_to_all | solution.py:120
  72.8 22.5 %copy-start.4 = (f32[31,1536]{1,0:T(8,128)S(1)}, f32[31,1536]{1,0:T(8,128)}, u32[]{:S(2)}) copy-start(f32[31,1536]{1,0:T(8,128)} %param.15) | copy-start | bytes 571396
  72.8 107.2 %all-gather.3.cloned.1.call-start = ((), (), s32[]{:S(2)}) async-start(), calls=%async_computation.1 | async-start | bytes 1597440 | tf_op jit(solution)/shard_map/all_gather | solution.py:91
  73.5 188.8 %all-gather.5.cloned.1.call-start = ((), (), s32[]{:S(2)}) async-start(), calls=%async_computation.2 | async-start | bytes 1597440 | tf_op jit(solution)/shard_map/all_gather | solution.py:92
  85.3 42.4 %collective-permute-start.2 = (bf16[256,1024]{1,0:T(8,128)(2,1)}, bf16[256,1024]{1,0:T(8,128)(2,1)S(1)}, u32[]{:S(2)}, u32[]{:S(2)}) collective-permute-start(bf16[256,1024]{1,0:T(8,128)(2,1)} %get-tuple-element.48), channel_id=1, source_target_pairs={{0,384},{8,392},{16,400},{24,408},{32,416},{40,424},{48,432},{56,4... | collective-permute-start | bytes 1572872 | tf_op jit(solution)/shard_map/ppermute | solution.py:10
  87.2 40.5 %collective-permute-start.1 = (bf16[256,1024]{1,0:T(8,128)(2,1)S(1)}, bf16[256,1024]{1,0:T(8,128)(2,1)S(1)}, u32[]{:S(2)}, u32[]{:S(2)}) collective-permute-start(bf16[256,1024]{1,0:T(8,128)(2,1)S(1)} %get-tuple-element.47), channel_id=1, source_target_pairs={{0,256},{8,264},{16,272},{24,280},{32,288},{40,296},{48,304},{56,3... | collective-permute-start | bytes 1572872 | tf_op jit(solution)/shard_map/ppermute | solution.py:10
  89.3 41.9 %collective-permute-start = (bf16[256,1024]{1,0:T(8,128)(2,1)S(1)}, bf16[256,1024]{1,0:T(8,128)(2,1)}, u32[]{:S(2)}, u32[]{:S(2)}) collective-permute-start(bf16[256,1024]{1,0:T(8,128)(2,1)S(1)} %get-tuple-element.46), channel_id=1, source_target_pairs={{0,128},{8,136},{16,144},{24,152},{32,160},{40,168},{48,176},{56,1... | collective-permute-start | bytes 1572872 | tf_op jit(solution)/shard_map/ppermute | solution.py:10
  96.4 36.3 %copy-start.11 = (s32[1024]{0:T(1024)S(1)}, s32[1024]{0:T(1024)}, u32[]{:S(2)}) copy-start(s32[1024]{0:T(1024)} %pad_clamp_fusion) | copy-start | bytes 12292
  127.7 3.5 copy-start.2
  127.7 3.5 copy-start.3
  308.1 22.4 %copy-start.14 = (f32[1536]{0:T(1024)S(1)}, f32[1536]{0:T(1024)}, u32[]{:S(2)}) copy-start(f32[1536]{0:T(1024)} %param.16) | copy-start | bytes 18436
  330.6 5.1 %copy-start = (bf16[1,1536,1536]{2,1,0:T(8,128)(2,1)S(1)}, bf16[1,1536,1536]{2,1,0:T(8,128)(2,1)}, u32[]{:S(2)}) copy-start(bf16[1,1536,1536]{2,1,0:T(8,128)(2,1)} %copy.34) | copy-start | bytes 14155780
  335.7 2.7 copy-start.5
  335.7 2.7 copy-start.6
  335.7 2.7 copy-start.7
  335.7 2.7 copy-start.8
  335.8 2.7 copy-start.9
  362.4 0.7 copy-start.12
Sparse Core Ops, SparseCore 0:
  76.7 103.2 all-gather.2
  183.1 79.2 all-gather.4
